TPU v7x, 256 devices: a whole 4x4x8 slice. The times are simulated.
256 devices in a mesh: dp: 32 (over y, x, core), mp: 8 (over z).
Axes of the slice: x: 4, y: 4, z: 8, core: 2. Of those that a mesh axis runs over, the one named last changes fastest.
Arguments:
- hidden: bfloat16 [16384, 4096], P('dp', 'mp'), may hold values from -50 to 50
- norm_gain: float32 [4096], replicated, may hold values from 0.1 to 1.9
- w_query: bfloat16 [4096, 4096], P(None, 'mp'), may hold values from -0.09375 to 0.09375
- w_out: bfloat16 [4096, 4096], P('mp'), may hold values from -0.09375 to 0.09375
- nb_keys: bfloat16 [256, 128, 4096], P('dp', None, 'mp'), may hold values from -250 to 250
- nb_values: bfloat16 [256, 128, 4096], P('dp', None, 'mp'), may hold values from -10 to 10
- neighbours: int32 [256, 2], P('dp'), may hold values from 0 to 255, as said below
- valid_spans: int32 [32], P('dp'), may hold values from 6 to 8, as said below
Outputs:
- mixed: float32 [16384, 4096], P('dp', 'mp')
Inputs may be any that keep to these rules, and one draw needn't show every extreme that they name: Block ids; block b is stored by index b // 8 of dp, its owner. The two neighbours of a span have different owners. The spans of one index of dp name one owner at most 2 times, and some owner is named exactly 2 times by the live spans of every index of dp. `valid_spans`: some index of dp has all 8 spans live.
All inputs are finite; a program needn't handle non-finite values.
Results may differ from a plain program's by a relative error of at most 0.0066.
Values may be sent and summed in bfloat16 or wider, within the bound.
No kernel may reach another device: no remote copies, remote signals or barrier semaphores. Data moves between devices by JAX's collectives and lax.ppermute only.
A program may use at most 128 MiB of HBM per device.

v0:
```python
import math
import jax
import jax.numpy as jnp
from jax import lax
from jax.sharding import PartitionSpec as P

HS = 128
SPAN = 64
eps = 1e-05


def shifted(block, axis, distance):
    devices = range(lax.axis_size(axis))
    route = [(i - distance, i) for i in devices if i - distance in devices]
    return lax.ppermute(block, axis, route)


def partial_attention(query_rows, key_rows, value_rows):
    inner_width = key_rows.shape[-1]
    head_count = inner_width // HS
    query_heads = query_rows.reshape(query_rows.shape[:-1] + (head_count, HS))
    key_heads = key_rows.reshape(key_rows.shape[:-1] + (head_count, HS))
    value_heads = value_rows.reshape(value_rows.shape[:-1] + (head_count, HS))
    factor = 1.0 / math.sqrt(HS)
    scores = (
        jnp.einsum(
            "...qhd,...khd->...qhk", query_heads, key_heads, preferred_element_type=jnp.float32
        )
        * factor
    )
    score_top = jnp.max(scores, axis=-1)
    weights = jnp.exp(scores - score_top[..., None])
    weight_sum = jnp.sum(weights, axis=-1)
    summed = jnp.einsum(
        "...qhk,...khd->...qhd",
        weights.astype(jnp.bfloat16),
        value_heads,
        preferred_element_type=jnp.float32,
    )
    part_out = (summed / weight_sum[..., None]).astype(jnp.bfloat16)
    return (part_out.reshape(part_out.shape[:-2] + (inner_width,)), score_top, weight_sum)


def combine(part_out, score_top, weight_sum):
    head_count = score_top.shape[-1]
    best_score = jnp.max(score_top, axis=1, keepdims=True)
    mix_weight = jnp.exp(score_top - best_score) * weight_sum
    widened = part_out.reshape(part_out.shape[:-1] + (head_count, HS)).astype(jnp.float32)
    merged = (
        jnp.sum(widened * mix_weight[..., None], axis=1) / jnp.sum(mix_weight, axis=1)[..., None]
    )
    return merged.reshape(merged.shape[:-2] + (head_count * HS,)).astype(jnp.bfloat16)


def shards(hidden, norm_gain, w_query, w_out, nb_keys, nb_values, neighbours, valid_spans):
    tok_rows = hidden.shape[0]
    span_dev = tok_rows // SPAN
    stored = nb_keys.shape[0]
    inner_width = w_query.shape[1]
    peer_count = lax.axis_size("dp")
    most_slots = max(2, (2 * span_dev + peer_count - 1) // peer_count)
    widened = lax.all_gather(hidden, "mp", axis=1, tiled=True).astype(jnp.float32)
    normed = (
        widened * lax.rsqrt(jnp.mean(widened * widened, axis=1, keepdims=True) + eps) * norm_gain
    ).astype(jnp.bfloat16)
    queries = jnp.dot(normed, w_query, preferred_element_type=jnp.float32).astype(jnp.bfloat16)
    following = shifted(queries[: SPAN - 1], "dp", -1)
    grouped = jnp.concatenate([queries[SPAN - 1 :], following], axis=0).reshape(
        span_dev, SPAN, inner_width
    )
    live_span = jnp.arange(span_dev, dtype=jnp.int32) < valid_spans[0]
    owners = (neighbours // stored).reshape(-1)
    slot_ids = (neighbours % stored).reshape(-1)
    is_live = jnp.repeat(live_span, 2)
    req_order = jnp.arange(owners.shape[0], dtype=jnp.int32)
    earlier = (
        (owners[:, None] == owners[None, :])
        & is_live[None, :]
        & (req_order[None, :] < req_order[:, None])
    )
    slot_rank = jnp.minimum(jnp.sum(earlier.astype(jnp.int32), axis=1), most_slots - 1)
    target = jnp.where(is_live, owners * most_slots + slot_rank, -1)
    slot_match = target[:, None] == jnp.arange(peer_count * most_slots, dtype=jnp.int32)[None, :]
    filled = jnp.any(slot_match, axis=0)
    request_table = jnp.where(
        filled, jnp.sum(jnp.where(slot_match, slot_ids[:, None], 0), axis=0), -1
    )
    request_table = request_table.reshape(peer_count, most_slots)
    source_span = jnp.sum(jnp.where(slot_match, req_order[:, None] // 2, 0), axis=0)
    sent_rows = grouped[source_span].reshape(peer_count, most_slots, SPAN, inner_width)
    wanted = lax.all_to_all(request_table, "dp", split_axis=0, concat_axis=0, tiled=True)
    asked = lax.all_to_all(sent_rows, "dp", split_axis=0, concat_axis=0, tiled=True)
    safe_ids = jnp.maximum(wanted, 0)
    result = partial_attention(asked, nb_keys[safe_ids], nb_values[safe_ids])
    part_back = lax.all_to_all(
        result[0].astype(jnp.float32), "dp", split_axis=0, concat_axis=0, tiled=True
    ).astype(jnp.bfloat16)
    top_back = lax.all_to_all(result[1], "dp", split_axis=0, concat_axis=0, tiled=True)
    sum_back = lax.all_to_all(result[2], "dp", split_axis=0, concat_axis=0, tiled=True)
    part_out = part_back[owners, slot_rank].reshape(span_dev, 2, SPAN, inner_width)
    score_top = top_back[owners, slot_rank].reshape(span_dev, 2, SPAN, -1)
    weight_sum = sum_back[owners, slot_rank].reshape(span_dev, 2, SPAN, -1)
    merged = combine(part_out, score_top, weight_sum)
    merged = jnp.where(live_span[:, None, None], merged, jnp.zeros_like(merged))
    flat_rows = merged.reshape(tok_rows, inner_width)
    previous = shifted(flat_rows[tok_rows - SPAN + 1 :], "dp", 1)
    placed = jnp.concatenate([previous, flat_rows[: tok_rows - SPAN + 1]], axis=0)
    head_terms = jnp.dot(placed, w_out, preferred_element_type=jnp.float32)
    summed = lax.psum_scatter(head_terms, "mp", scatter_dimension=1, tiled=True)
    return hidden.astype(jnp.float32) + summed


def solution(mesh):
    placed = (
        P("dp", "mp"),
        P(),
        P(None, "mp"),
        P("mp", None),
        P("dp", None, "mp"),
        P("dp", None, "mp"),
        P("dp", None),
        P("dp"),
    )
    return jax.shard_map(
        shards, mesh=mesh, in_specs=placed, out_specs=P("dp", "mp"), check_vma=False
    )
```

profile of v0, /device:TPU:1, one launch (start us, length us, event | category | flops | bytes accessed | tf_op | source)
XLA Modules:
  0.0 369.9 jit_solution(1386096142998444938)
XLA Ops:
  10.2 8.6 %all-to-all-start = ((s32[32,1,2]{2,1,0:T(1,128)}), s32[32,1,2]{2,1,0:T(1,128)S(1)}, u32[]{:S(2)}, u32[]{:S(2)}) async-start(s32[32,1,2]{2,1,0:T(1,128)} %bitcast.1), calls=%async_computation | async-start | bytes 32768 | tf_op jit(solution)/shard_map/all_to_all | solution.py:91
  18.8 48.7 %all-gather.2.cloned.1.call-done = bf16[512,4096]{1,0:T(8,128)(2,1)} async-done(((bf16[512,512]{1,0:T(8,128)(2,1)}), bf16[512,4096]{1,0:T(8,128)(2,1)}) %all-gather.2.cloned.1.call-update) | async-done | bytes 4194320 | tf_op jit(solution)/shard_map/all_gather | solution.py:62
  67.5 3.1 fusion
  70.6 5.9 %fusion.24 = bf16[512,512]{1,0:T(8,128)(2,1)S(1)} fusion(bf16[4096,512]{1,0:T(8,128)(2,1)} %param.10, bf16[512,4096]{1,0:T(8,128)(2,1)} %all-gather.2.cloned.1.call-done, f32[4096]{0:T(1024)} %param.9, f32[512]{0:T(512)S(1)} %add_rsqrt_fusion), kind=kOutput, calls=%fused_computation.32 | convolution fusion | flops 2156134400 | bytes 8931328 | tf_op jit(solution)/shard_map/dot_general | solution.py:66
  76.5 2.8 collective-permute-start
  79.4 2.9 collective-permute-done
  82.3 2.8 gather_fusion.2
  85.1 8.7 %all-to-all-start.1 = ((bf16[32,2,64,512]{3,2,1,0:T(8,128)(2,1)}), bf16[32,2,64,512]{3,2,1,0:T(8,128)(2,1)}, u32[]{:S(2)}, u32[]{:S(2)}) async-start(bf16[32,2,64,512]{3,2,1,0:T(8,128)(2,1)} %bitcast.69), calls=%async_computation.1 | async-start | bytes 8388608 | tf_op jit(solution)/shard_map/all_to_all | solution.py:92
  93.9 5.3 %gather_fusion.1 = bf16[64,128,512]{2,1,0:T(8,128)(2,1)} fusion(bf16[8,128,512]{2,1,0:T(8,128)(2,1)S(1)} %copy-done, s32[1024]{0:T(1024)S(1)} %pad_clamp_fusion.1), kind=kCustom, calls=%fused_computation.1 | custom fusion | bytes 16777472 | tf_op jit(solution)/shard_map/gather | solution.py:94
  99.3 12.6 %reshape.223 = bf16[32,2,128,4,128]{4,3,2,1,0:T(4,128)(2,1)} reshape(bf16[64,128,512]{2,1,0:T(8,128)(2,1)} %gather_fusion.1) | data formatting | bytes 16777216 | tf_op jit(solution)/shard_map/reshape | solution.py:22
  111.9 5.3 %gather_fusion = bf16[64,128,512]{2,1,0:T(8,128)(2,1)} fusion(bf16[8,128,512]{2,1,0:T(8,128)(2,1)S(1)} %copy-done.2, s32[1024]{0:T(1024)S(1)} %pad_clamp_fusion.1), kind=kCustom, calls=%fused_computation | custom fusion | bytes 16777472 | tf_op jit(solution)/shard_map/gather | solution.py:94
  117.3 12.5 %reshape.222 = bf16[32,2,128,4,128]{4,3,2,1,0:T(4,128)(2,1)} reshape(bf16[64,128,512]{2,1,0:T(8,128)(2,1)} %gather_fusion) | data formatting | bytes 16777216 | tf_op jit(solution)/shard_map/reshape | solution.py:23
  129.8 14.7 %all-to-all-done.1 = bf16[32,2,64,512]{3,2,1,0:T(8,128)(2,1)} async-done(((bf16[32,2,64,512]{3,2,1,0:T(8,128)(2,1)}), bf16[32,2,64,512]{3,2,1,0:T(8,128)(2,1)}, u32[]{:S(2)}, u32[]{:S(2)}) %all-to-all-start.1) | async-done | bytes 4194336 | tf_op jit(solution)/shard_map/all_to_all | solution.py:92
  144.4 11.0 %bitcast_reduce_fusion = (f32[32,2,64,4]{2,3,1,0:T(4,128)S(1)}, f32[32,2,4,128,64]{3,4,2,1,0:T(8,128)}) fusion(bf16[32,2,128,4,128]{4,3,2,1,0:T(4,128)(2,1)} %reshape.223, bf16[32,2,64,512]{3,2,1,0:T(8,128)(2,1)} %all-to-all-done.1), kind=kOutput, calls=%fused_computation.15 | convolution fusion | flops 541048832 | bytes 21037056 | tf_op jit(solution)/shard_map/...qhd,...khd->...qhk/dot_general | solution.py:26
  156.2 7.1 %all-to-all-start.3 = ((f32[32,1,512]{2,1,0:T(1,128)}), f32[32,1,512]{2,1,0:T(1,128)S(1)}, u32[]{:S(2)}, u32[]{:S(2)}) async-start(f32[32,1,512]{2,1,0:T(1,128)} %reshape.289), calls=%async_computation.3 | async-start | bytes 131072 | tf_op jit(solution)/shard_map/all_to_all | solution.py:98
  163.3 6.9 %fusion.9 = f32[32,2,64,4]{2,3,1,0:T(4,128)S(1)} fusion(f32[32,2,4,128,64]{3,4,2,1,0:T(8,128)} %get-tuple-element.12, f32[32,2,64,4]{2,3,1,0:T(4,128)S(1)} %get-tuple-element.11), kind=kLoop, calls=%fused_computation.22 | loop fusion | flops 6275072 | bytes 8519680 | tf_op jit(solution)/shard_map/reduce_sum | solution.py:33
  171.0 7.5 %all-to-all-start.4 = ((f32[32,1,512]{2,1,0:T(1,128)}), f32[32,1,512]{2,1,0:T(1,128)S(1)}, u32[]{:S(2)}, u32[]{:S(2)}) async-start(f32[32,1,512]{2,1,0:T(1,128)} %reshape.287), calls=%async_computation.4 | async-start | bytes 131072 | tf_op jit(solution)/shard_map/all_to_all | solution.py:99
  178.5 9.0 %convert_bitcast_fusion = bf16[32,2,4,8,8,128]{5,4,3,2,1,0:T(8,128)(2,1)S(1)} fusion(f32[32,2,64,4]{2,3,1,0:T(4,128)S(1)} %fusion.9, bf16[32,2,128,4,128]{4,3,2,1,0:T(4,128)(2,1)} %reshape.222, f32[32,2,4,128,64]{3,4,2,1,0:T(8,128)} %get-tuple-element.12, f32[32,2,64,4]{2,3,1,0:T(4,128)S(1)} %get-tuple-element.11), kind=kOutput, calls=%fused_computation.21 | convolution fusion | flops 547356672 | bytes 21102592 | tf_op jit(solution)/shard_map/...qhk,...khd->...qhd/dot_general | solution.py:34
  190.2 7.4 %all-to-all-start.2 = ((bf16[32,2,64,512]{3,2,1,0:T(8,128)(2,1)}), bf16[32,2,64,512]{3,2,1,0:T(8,128)(2,1)}, u32[]{:S(2)}, u32[]{:S(2)}) async-start(bf16[32,2,64,512]{3,2,1,0:T(8,128)(2,1)} %bitcast.68), calls=%async_computation.2 | async-start | bytes 8388608 | tf_op jit(solution)/shard_map/all_to_all | solution.py:95
  202.8 45.5 %all-to-all-done.2 = bf16[32,2,64,512]{3,2,1,0:T(8,128)(2,1)} async-done(((bf16[32,2,64,512]{3,2,1,0:T(8,128)(2,1)}), bf16[32,2,64,512]{3,2,1,0:T(8,128)(2,1)}, u32[]{:S(2)}, u32[]{:S(2)}) %all-to-all-start.2) | async-done | bytes 4194336 | tf_op jit(solution)/shard_map/all_to_all | solution.py:95
  248.3 2.8 gather_fusion.3
  255.4 4.3 %collective-permute-start.1 = (bf16[63,512]{1,0:T(8,128)(2,1)S(1)}, bf16[63,512]{1,0:T(8,128)(2,1)S(1)}, u32[]{:S(2)}, u32[]{:S(2)}) collective-permute-start(bf16[63,512]{1,0:T(8,128)(2,1)S(1)} %slice.30), channel_id=1, source_target_pairs={{0,8},{8,16},{16,24},{24,32},{32,40},{40,48},{48,56},{56,64},{64,7... | collective-permute-start | bytes 193544 | tf_op jit(solution)/shard_map/ppermute | solution.py:15
  261.1 5.6 %fusion.27 = f32[512,4096]{1,0:T(8,128)} fusion(bf16[512,4096]{1,0:T(8,128)(2,1)S(1)} %copy-done.3, bf16[449,512]{1,0:T(8,128)(2,1)S(1)} %slice.31, bf16[63,512]{1,0:T(8,128)(2,1)S(1)} %collective-permute-done.1), kind=kOutput, calls=%fused_computation.37 | convolution fusion | flops 2148532224 | bytes 13107200 | tf_op jit(solution)/shard_map/dot_general | solution.py:108
  266.7 94.0 %reduce-scatter.2.cloned.1.call-done = f32[512,512]{1,0:T(8,128)} async-done(((f32[512,4096]{1,0:T(8,128)}), f32[512,512]{1,0:T(8,128)}) %reduce-scatter.2.cloned.1.call-update) | async-done | bytes 1048592 | tf_op jit(solution)/shard_map/reduce_scatter | solution.py:109
  (66 shorter events, 20.6 us)
Async XLA Ops:
  6.5 87.4 %copy-start = (bf16[8,128,512]{2,1,0:T(8,128)(2,1)S(1)}, bf16[8,128,512]{2,1,0:T(8,128)(2,1)}, u32[]{:S(2)}) copy-start(bf16[8,128,512]{2,1,0:T(8,128)(2,1)} %param.12) | copy-start | bytes 3145732
  6.5 61.0 %all-gather.2.cloned.1.call-start = ((), (), s32[]{:S(2)}) async-start(), calls=%async_computation.6 | async-start | bytes 4718592 | tf_op jit(solution)/shard_map/all_gather | solution.py:62
  10.2 74.9 %all-to-all-start = ((s32[32,1,2]{2,1,0:T(1,128)}), s32[32,1,2]{2,1,0:T(1,128)S(1)}, u32[]{:S(2)}, u32[]{:S(2)}) async-start(s32[32,1,2]{2,1,0:T(1,128)} %bitcast.1), calls=%async_computation | async-start | bytes 32768 | tf_op jit(solution)/shard_map/all_to_all | solution.py:91
  76.5 5.8 %collective-permute-start = (bf16[63,512]{1,0:T(8,128)(2,1)S(1)}, bf16[63,512]{1,0:T(8,128)(2,1)S(1)}, u32[]{:S(2)}, u32[]{:S(2)}) collective-permute-start(bf16[63,512]{1,0:T(8,128)(2,1)S(1)} %slice.29), channel_id=1, source_target_pairs={{8,0},{16,8},{24,16},{32,24},{40,32},{48,40},{56,48},{64,56},{72,6... | collective-permute-start | bytes 193544 | tf_op jit(solution)/shard_map/ppermute | solution.py:15
  85.1 59.4 %all-to-all-start.1 = ((bf16[32,2,64,512]{3,2,1,0:T(8,128)(2,1)}), bf16[32,2,64,512]{3,2,1,0:T(8,128)(2,1)}, u32[]{:S(2)}, u32[]{:S(2)}) async-start(bf16[32,2,64,512]{3,2,1,0:T(8,128)(2,1)} %bitcast.69), calls=%async_computation.1 | async-start | bytes 8388608 | tf_op jit(solution)/shard_map/all_to_all | solution.py:92
  99.3 12.6 %copy-start.2 = (bf16[8,128,512]{2,1,0:T(8,128)(2,1)S(1)}, bf16[8,128,512]{2,1,0:T(8,128)(2,1)}, u32[]{:S(2)}) copy-start(bf16[8,128,512]{2,1,0:T(8,128)(2,1)} %param.13) | copy-start | bytes 3145732
  156.2 14.8 %all-to-all-start.3 = ((f32[32,1,512]{2,1,0:T(1,128)}), f32[32,1,512]{2,1,0:T(1,128)S(1)}, u32[]{:S(2)}, u32[]{:S(2)}) async-start(f32[32,1,512]{2,1,0:T(1,128)} %reshape.289), calls=%async_computation.3 | async-start | bytes 131072 | tf_op jit(solution)/shard_map/all_to_all | solution.py:98
  171.0 19.2 %all-to-all-start.4 = ((f32[32,1,512]{2,1,0:T(1,128)}), f32[32,1,512]{2,1,0:T(1,128)S(1)}, u32[]{:S(2)}, u32[]{:S(2)}) async-start(f32[32,1,512]{2,1,0:T(1,128)} %reshape.287), calls=%async_computation.4 | async-start | bytes 131072 | tf_op jit(solution)/shard_map/all_to_all | solution.py:99
  190.2 58.1 %all-to-all-start.2 = ((bf16[32,2,64,512]{3,2,1,0:T(8,128)(2,1)}), bf16[32,2,64,512]{3,2,1,0:T(8,128)(2,1)}, u32[]{:S(2)}, u32[]{:S(2)}) async-start(bf16[32,2,64,512]{3,2,1,0:T(8,128)(2,1)} %bitcast.68), calls=%async_computation.2 | async-start | bytes 8388608 | tf_op jit(solution)/shard_map/all_to_all | solution.py:95
  197.7 163.0 %reduce-scatter.2.cloned.1.call-start = ((), (), s32[]{:S(2)}) async-start(), calls=%async_computation.7 | async-start | bytes 9437184 | tf_op jit(solution)/shard_map/reduce_scatter | solution.py:109
  251.9 9.2 %copy-start.3 = (bf16[512,4096]{1,0:T(8,128)(2,1)S(1)}, bf16[512,4096]{1,0:T(8,128)(2,1)}, u32[]{:S(2)}) copy-start(bf16[512,4096]{1,0:T(8,128)(2,1)} %param.11) | copy-start | bytes 12582916
  255.4 5.6 %collective-permute-start.1 = (bf16[63,512]{1,0:T(8,128)(2,1)S(1)}, bf16[63,512]{1,0:T(8,128)(2,1)S(1)}, u32[]{:S(2)}, u32[]{:S(2)}) collective-permute-start(bf16[63,512]{1,0:T(8,128)(2,1)S(1)} %slice.30), channel_id=1, source_target_pairs={{0,8},{8,16},{16,24},{24,32},{32,40},{40,48},{48,56},{56,64},{64,7... | collective-permute-start | bytes 193544 | tf_op jit(solution)/shard_map/ppermute | solution.py:15
  259.8 100.9 %copy-start.4 = (bf16[512,512]{1,0:T(8,128)(2,1)S(1)}, bf16[512,512]{1,0:T(8,128)(2,1)}, u32[]{:S(2)}) copy-start(bf16[512,512]{1,0:T(8,128)(2,1)} %param.8) | copy-start | bytes 1572868
  261.1 102.0 %copy-start.1 = (bf16[8,128,512]{2,1,0:T(8,128)(2,1)S(1)}, bf16[8,128,512]{2,1,0:T(8,128)(2,1)}, u32[]{:S(2)}) copy-start(bf16[8,128,512]{2,1,0:T(8,128)(2,1)} %param.12) | copy-start | bytes 3145732
Sparse Core Ops, SparseCore 0:
  9.1 58.3 all-gather.1
  266.8 93.8 reduce-scatter.1
where the time goes:
time: 371 us; the launch traced here: 370 us
  waiting for transfers between devices  208 us (56%)
  local copies, waits for them, and re-layouts  51.2 us (14%)
  starting transfers between devices  46.4 us (13%)
  matrix products  31.4 us (8%)
  other arithmetic  18.7 us (5%)
  between operations  14.3 us (4%)
    reduce_scatter x1, waiting for transfers between devices, shards(): summed = lax.psum_scatter(head_terms, 'mp', scatter_dimension=1, tiled=True)  94 us
    all_gather x1, waiting for transfers between devices, shards(): lax.all_gather(hidden, 'mp', axis=1, tiled=True).astype(jnp.float32)  48.7 us
    all_to_all x1, waiting for transfers between devices, shards(): lax.all_to_all(result[0].astype(jnp.float32), 'dp', split_axis=0, concat_...  45.5 us
    all_to_all x1, waiting for transfers between devices, shards(): lax.all_to_all(sent_rows, 'dp', split_axis=0, concat_axis=0, tiled=True)  14.7 us
    reshape x1, local copies, waits for them, and re-layouts, partial_attention(): key_heads = key_rows.reshape(key_rows.shape[:-1] + (head_count, HS))  12.6 us
    reshape x1, local copies, waits for them, and re-layouts, partial_attention(): value_heads = value_rows.reshape(value_rows.shape[:-1] + (head_count, HS))  12.5 us
    dot_general x1, matrix products, partial_attention(): jnp.einsum('...qhd,...khd->...qhk', query_heads, key_heads, preferred_ele...  11 us
    gather x2, local copies, waits for them, and re-layouts, shards(): result = partial_attention(asked, nb_keys[safe_ids], nb_values[safe_ids])  10.7 us
  transfers between devices with their start and end apart: 9, of which 6 were waited for; matrix products, arithmetic and copies ran while one was open for 20% of the time, Pallas kernels for 0%

commit v1 on v0

--- a/solution.py
+++ b/solution.py
@@ -59,7 +59,9 @@
     inner_width = w_query.shape[1]
     peer_count = lax.axis_size("dp")
     most_slots = max(2, (2 * span_dev + peer_count - 1) // peer_count)
-    widened = lax.all_gather(hidden, "mp", axis=1, tiled=True).astype(jnp.float32)
+    widened = jnp.concatenate(
+        lax.all_to_all(jnp.stack([hidden] * lax.axis_size("mp")), "mp", 0, 0), axis=1
+    ).astype(jnp.float32)
     normed = (
         widened * lax.rsqrt(jnp.mean(widened * widened, axis=1, keepdims=True) + eps) * norm_gain
     ).astype(jnp.bfloat16)

time: 371 us -> 424 us (1.14)
  waiting for transfers between devices: 208 us -> 251 us
  starting transfers between devices: 46.4 us -> 54.1 us
    all_to_all x0 -> x1, waiting for transfers between devices: none -> 94.6 us  [shards(): lax.all_to_all(jnp.stack([hidden] * lax.axis_size('mp')), 'mp', 0, 0)]
    all_gather x1 -> x0, waiting for transfers between devices: 48.7 us -> none  [shards(): lax.all_gather(hidden, 'mp', axis=1, tiled=True).astype(jnp.float32)]
    all_to_all x0 -> x1, starting transfers between devices: none -> 9 us  [shards(): lax.all_to_all(jnp.stack([hidden] * lax.axis_size('mp')), 'mp', 0, 0)]
  transfers between devices with their start and end apart: 9 -> 9, of which waited for: 6 -> 6; matrix products, arithmetic and copies ran while one was open for 20% -> 17% of each run, Pallas kernels for 0% -> 0%
where the time goes in v1:
time: 424 us; the launch traced here: 423 us
  waiting for transfers between devices  251 us (59%)
  local copies, waits for them, and re-layouts  54.9 us (13%)
  starting transfers between devices  54.1 us (13%)
  matrix products  28 us (7%)
  other arithmetic  21 us (5%)
  between operations  14.4 us (3%)
    all_to_all x1, waiting for transfers between devices, shards(): lax.all_to_all(jnp.stack([hidden] * lax.axis_size('mp')), 'mp', 0, 0)  94.6 us
    reduce_scatter x1, waiting for transfers between devices, shards(): summed = lax.psum_scatter(head_terms, 'mp', scatter_dimension=1, tiled=True)  91.5 us
    all_to_all x1, waiting for transfers between devices, shards(): lax.all_to_all(result[0].astype(jnp.float32), 'dp', split_axis=0, concat_...  45.5 us
    all_to_all x1, waiting for transfers between devices, shards(): lax.all_to_all(sent_rows, 'dp', split_axis=0, concat_axis=0, tiled=True)  14.7 us
    reshape x1, local copies, waits for them, and re-layouts, partial_attention(): key_heads = key_rows.reshape(key_rows.shape[:-1] + (head_count, HS))  12.6 us
    reshape x1, local copies, waits for them, and re-layouts, partial_attention(): value_heads = value_rows.reshape(value_rows.shape[:-1] + (head_count, HS))  12.5 us
    dot_general x1, matrix products, partial_attention(): jnp.einsum('...qhd,...khd->...qhk', query_heads, key_heads, preferred_ele...  11 us
    gather x2, local copies, waits for them, and re-layouts, shards(): result = partial_attention(asked, nb_keys[safe_ids], nb_values[safe_ids])  10.7 us
  transfers between devices with their start and end apart: 9, of which 6 were waited for; matrix products, arithmetic and copies ran while one was open for 17% of the time, Pallas kernels for 0%

profile of v1, /device:TPU:1, one launch (start us, length us, event | category | flops | bytes accessed | tf_op | source)
XLA Modules:
  0.0 423.2 jit_solution(6970384313722825568)
XLA Ops:
  10.2 9.0 %all-to-all-start.1 = ((bf16[8,512,512]{1,2,0:T(8,128)(2,1)}), bf16[8,512,512]{1,2,0:T(8,128)(2,1)}, u32[]{:S(2)}, u32[]{:S(2)}) async-start(bf16[8,512,512]{1,2,0:T(8,128)(2,1)} %stack.2), calls=%async_computation.1 | async-start | bytes 8388608 | tf_op jit(solution)/shard_map/all_to_all | solution.py:63
  21.5 94.6 %all-to-all-done.1 = bf16[8,512,512]{1,2,0:T(8,128)(2,1)} async-done(((bf16[8,512,512]{1,2,0:T(8,128)(2,1)}), bf16[8,512,512]{1,2,0:T(8,128)(2,1)}, u32[]{:S(2)}, u32[]{:S(2)}) %all-to-all-start.1) | async-done | bytes 4194336 | tf_op jit(solution)/shard_map/all_to_all | solution.py:63
  116.1 7.6 %all-to-all-start = ((s32[32,1,2]{2,1,0:T(1,128)}), s32[32,1,2]{2,1,0:T(1,128)S(1)}, u32[]{:S(2)}, u32[]{:S(2)}) async-start(s32[32,1,2]{2,1,0:T(1,128)} %bitcast.1), calls=%async_computation | async-start | bytes 32768 | tf_op jit(solution)/shard_map/all_to_all | solution.py:93
  123.7 3.3 multiply_reduce_fusion
  127.0 2.8 fusion.1
  134.5 3.3 collective-permute-done
  137.8 2.8 gather_fusion.2
  140.6 9.0 %all-to-all-start.2 = ((bf16[32,2,64,512]{3,2,1,0:T(8,128)(2,1)}), bf16[32,2,64,512]{3,2,1,0:T(8,128)(2,1)}, u32[]{:S(2)}, u32[]{:S(2)}) async-start(bf16[32,2,64,512]{3,2,1,0:T(8,128)(2,1)} %bitcast.78), calls=%async_computation.2 | async-start | bytes 8388608 | tf_op jit(solution)/shard_map/all_to_all | solution.py:94
  149.8 5.3 %gather_fusion.1 = bf16[64,128,512]{2,1,0:T(8,128)(2,1)} fusion(bf16[8,128,512]{2,1,0:T(8,128)(2,1)S(1)} %copy-done, s32[1024]{0:T(1024)S(1)} %pad_clamp_fusion.1), kind=kCustom, calls=%fused_computation.1 | custom fusion | bytes 16777472 | tf_op jit(solution)/shard_map/gather | solution.py:96
  155.1 12.6 %reshape.229 = bf16[32,2,128,4,128]{4,3,2,1,0:T(4,128)(2,1)} reshape(bf16[64,128,512]{2,1,0:T(8,128)(2,1)} %gather_fusion.1) | data formatting | bytes 16777216 | tf_op jit(solution)/shard_map/reshape | solution.py:22
  167.7 5.3 %gather_fusion = bf16[64,128,512]{2,1,0:T(8,128)(2,1)} fusion(bf16[8,128,512]{2,1,0:T(8,128)(2,1)S(1)} %copy-done.2, s32[1024]{0:T(1024)S(1)} %pad_clamp_fusion.1), kind=kCustom, calls=%fused_computation | custom fusion | bytes 16777472 | tf_op jit(solution)/shard_map/gather | solution.py:96
  173.1 12.5 %reshape.228 = bf16[32,2,128,4,128]{4,3,2,1,0:T(4,128)(2,1)} reshape(bf16[64,128,512]{2,1,0:T(8,128)(2,1)} %gather_fusion) | data formatting | bytes 16777216 | tf_op jit(solution)/shard_map/reshape | solution.py:23
  185.6 14.7 %all-to-all-done.2 = bf16[32,2,64,512]{3,2,1,0:T(8,128)(2,1)} async-done(((bf16[32,2,64,512]{3,2,1,0:T(8,128)(2,1)}), bf16[32,2,64,512]{3,2,1,0:T(8,128)(2,1)}, u32[]{:S(2)}, u32[]{:S(2)}) %all-to-all-start.2) | async-done | bytes 4194336 | tf_op jit(solution)/shard_map/all_to_all | solution.py:94
  200.3 11.0 %bitcast_reduce_fusion = (f32[32,2,64,4]{2,3,1,0:T(4,128)S(1)}, f32[32,2,4,128,64]{3,4,2,1,0:T(8,128)}) fusion(bf16[32,2,128,4,128]{4,3,2,1,0:T(4,128)(2,1)} %reshape.229, bf16[32,2,64,512]{3,2,1,0:T(8,128)(2,1)} %all-to-all-done.2), kind=kOutput, calls=%fused_computation.13 | convolution fusion | flops 541048832 | bytes 21037056 | tf_op jit(solution)/shard_map/...qhd,...khd->...qhk/dot_general | solution.py:26
  212.1 7.1 %all-to-all-start.4 = ((f32[32,1,512]{2,1,0:T(1,128)}), f32[32,1,512]{2,1,0:T(1,128)S(1)}, u32[]{:S(2)}, u32[]{:S(2)}) async-start(f32[32,1,512]{2,1,0:T(1,128)} %reshape.296), calls=%async_computation.4 | async-start | bytes 131072 | tf_op jit(solution)/shard_map/all_to_all | solution.py:100
  219.2 6.9 %fusion.8 = f32[32,2,64,4]{2,3,1,0:T(4,128)S(1)} fusion(f32[32,2,4,128,64]{3,4,2,1,0:T(8,128)} %get-tuple-element.12, f32[32,2,64,4]{2,3,1,0:T(4,128)S(1)} %get-tuple-element.11), kind=kLoop, calls=%fused_computation.21 | loop fusion | flops 6275072 | bytes 8519680 | tf_op jit(solution)/shard_map/reduce_sum | solution.py:33
  226.8 7.5 %all-to-all-start.5 = ((f32[32,1,512]{2,1,0:T(1,128)}), f32[32,1,512]{2,1,0:T(1,128)S(1)}, u32[]{:S(2)}, u32[]{:S(2)}) async-start(f32[32,1,512]{2,1,0:T(1,128)} %reshape.294), calls=%async_computation.5 | async-start | bytes 131072 | tf_op jit(solution)/shard_map/all_to_all | solution.py:101
  234.3 9.0 %convert_bitcast_fusion = bf16[32,2,4,8,8,128]{5,4,3,2,1,0:T(8,128)(2,1)S(1)} fusion(f32[32,2,64,4]{2,3,1,0:T(4,128)S(1)} %fusion.8, bf16[32,2,128,4,128]{4,3,2,1,0:T(4,128)(2,1)} %reshape.228, f32[32,2,4,128,64]{3,4,2,1,0:T(8,128)} %get-tuple-element.12, f32[32,2,64,4]{2,3,1,0:T(4,128)S(1)} %get-tuple-element.11), kind=kOutput, calls=%fused_computation.19 | convolution fusion | flops 547356672 | bytes 21102592 | tf_op jit(solution)/shard_map/...qhk,...khd->...qhd/dot_general | solution.py:34
  246.1 7.4 %all-to-all-start.3 = ((bf16[32,2,64,512]{3,2,1,0:T(8,128)(2,1)}), bf16[32,2,64,512]{3,2,1,0:T(8,128)(2,1)}, u32[]{:S(2)}, u32[]{:S(2)}) async-start(bf16[32,2,64,512]{3,2,1,0:T(8,128)(2,1)} %bitcast.77), calls=%async_computation.3 | async-start | bytes 8388608 | tf_op jit(solution)/shard_map/all_to_all | solution.py:97
  258.7 45.5 %all-to-all-done.3 = bf16[32,2,64,512]{3,2,1,0:T(8,128)(2,1)} async-done(((bf16[32,2,64,512]{3,2,1,0:T(8,128)(2,1)}), bf16[32,2,64,512]{3,2,1,0:T(8,128)(2,1)}, u32[]{:S(2)}, u32[]{:S(2)}) %all-to-all-start.3) | async-done | bytes 4194336 | tf_op jit(solution)/shard_map/all_to_all | solution.py:97
  304.2 2.8 gather_fusion.3
  311.3 4.3 %collective-permute-start.1 = (bf16[63,512]{1,0:T(8,128)(2,1)S(1)}, bf16[63,512]{1,0:T(8,128)(2,1)S(1)}, u32[]{:S(2)}, u32[]{:S(2)}) collective-permute-start(bf16[63,512]{1,0:T(8,128)(2,1)S(1)} %slice.30), channel_id=1, source_target_pairs={{0,8},{8,16},{16,24},{24,32},{32,40},{40,48},{48,56},{56,64},{64,7... | collective-permute-start | bytes 193544 | tf_op jit(solution)/shard_map/ppermute | solution.py:15
  316.9 5.6 %fusion.19 = f32[512,4096]{1,0:T(8,128)} fusion(bf16[512,4096]{1,0:T(8,128)(2,1)S(1)} %copy-done.3, bf16[449,512]{1,0:T(8,128)(2,1)S(1)} %slice.31, bf16[63,512]{1,0:T(8,128)(2,1)S(1)} %collective-permute-done.1), kind=kOutput, calls=%fused_computation.33 | convolution fusion | flops 2148532224 | bytes 13107200 | tf_op jit(solution)/shard_map/dot_general | solution.py:110
  322.5 91.5 %reduce-scatter.2.cloned.1.call-done = f32[512,512]{1,0:T(8,128)} async-done(((f32[512,4096]{1,0:T(8,128)}), f32[512,512]{1,0:T(8,128)}) %reduce-scatter.2.cloned.1.call-update) | async-done | bytes 1048592 | tf_op jit(solution)/shard_map/reduce_scatter | solution.py:111
  (74 shorter events, 27.4 us)
Async XLA Ops:
  6.5 143.2 %copy-start = (bf16[8,128,512]{2,1,0:T(8,128)(2,1)S(1)}, bf16[8,128,512]{2,1,0:T(8,128)(2,1)}, u32[]{:S(2)}) copy-start(bf16[8,128,512]{2,1,0:T(8,128)(2,1)} %param.12) | copy-start | bytes 3145732
  6.5 13.5 %copy-start.6 = (s32[8,2]{0,1:T(2,128)S(1)}, s32[8,2]{0,1:T(2,128)}, u32[]{:S(2)}) copy-start(s32[8,2]{0,1:T(2,128)} %param.14) | copy-start | bytes 196
  7.9 119.1 %copy-start.5 = (f32[4096]{0:T(1024)S(1)}, f32[4096]{0:T(1024)}, u32[]{:S(2)}) copy-start(f32[4096]{0:T(1024)} %param.9) | copy-start | bytes 49156
  10.2 105.9 %all-to-all-start.1 = ((bf16[8,512,512]{1,2,0:T(8,128)(2,1)}), bf16[8,512,512]{1,2,0:T(8,128)(2,1)}, u32[]{:S(2)}, u32[]{:S(2)}) async-start(bf16[8,512,512]{1,2,0:T(8,128)(2,1)} %stack.2), calls=%async_computation.1 | async-start | bytes 8388608 | tf_op jit(solution)/shard_map/all_to_all | solution.py:63
  116.1 24.5 %all-to-all-start = ((s32[32,1,2]{2,1,0:T(1,128)}), s32[32,1,2]{2,1,0:T(1,128)S(1)}, u32[]{:S(2)}, u32[]{:S(2)}) async-start(s32[32,1,2]{2,1,0:T(1,128)} %bitcast.1), calls=%async_computation | async-start | bytes 32768 | tf_op jit(solution)/shard_map/all_to_all | solution.py:93
  123.7 6.1 %copy-start.7 = (bf16[4096,512]{1,0:T(8,128)(2,1)S(1)}, bf16[4096,512]{1,0:T(8,128)(2,1)}, u32[]{:S(2)}) copy-start(bf16[4096,512]{1,0:T(8,128)(2,1)} %param.10) | copy-start | bytes 12582916
  132.2 5.6 %collective-permute-start = (bf16[63,512]{1,0:T(8,128)(2,1)S(1)}, bf16[63,512]{1,0:T(8,128)(2,1)S(1)}, u32[]{:S(2)}, u32[]{:S(2)}) collective-permute-start(bf16[63,512]{1,0:T(8,128)(2,1)S(1)} %slice.29), channel_id=1, source_target_pairs={{8,0},{16,8},{24,16},{32,24},{40,32},{48,40},{56,48},{64,56},{72,6... | collective-permute-start | bytes 193544 | tf_op jit(solution)/shard_map/ppermute | solution.py:15
  140.6 59.7 %all-to-all-start.2 = ((bf16[32,2,64,512]{3,2,1,0:T(8,128)(2,1)}), bf16[32,2,64,512]{3,2,1,0:T(8,128)(2,1)}, u32[]{:S(2)}, u32[]{:S(2)}) async-start(bf16[32,2,64,512]{3,2,1,0:T(8,128)(2,1)} %bitcast.78), calls=%async_computation.2 | async-start | bytes 8388608 | tf_op jit(solution)/shard_map/all_to_all | solution.py:94
  155.1 12.6 %copy-start.2 = (bf16[8,128,512]{2,1,0:T(8,128)(2,1)S(1)}, bf16[8,128,512]{2,1,0:T(8,128)(2,1)}, u32[]{:S(2)}) copy-start(bf16[8,128,512]{2,1,0:T(8,128)(2,1)} %param.13) | copy-start | bytes 3145732
  212.1 14.8 %all-to-all-start.4 = ((f32[32,1,512]{2,1,0:T(1,128)}), f32[32,1,512]{2,1,0:T(1,128)S(1)}, u32[]{:S(2)}, u32[]{:S(2)}) async-start(f32[32,1,512]{2,1,0:T(1,128)} %reshape.296), calls=%async_computation.4 | async-start | bytes 131072 | tf_op jit(solution)/shard_map/all_to_all | solution.py:100
  226.8 19.2 %all-to-all-start.5 = ((f32[32,1,512]{2,1,0:T(1,128)}), f32[32,1,512]{2,1,0:T(1,128)S(1)}, u32[]{:S(2)}, u32[]{:S(2)}) async-start(f32[32,1,512]{2,1,0:T(1,128)} %reshape.294), calls=%async_computation.5 | async-start | bytes 131072 | tf_op jit(solution)/shard_map/all_to_all | solution.py:101
  246.1 58.1 %all-to-all-start.3 = ((bf16[32,2,64,512]{3,2,1,0:T(8,128)(2,1)}), bf16[32,2,64,512]{3,2,1,0:T(8,128)(2,1)}, u32[]{:S(2)}, u32[]{:S(2)}) async-start(bf16[32,2,64,512]{3,2,1,0:T(8,128)(2,1)} %bitcast.77), calls=%async_computation.3 | async-start | bytes 8388608 | tf_op jit(solution)/shard_map/all_to_all | solution.py:97
  253.5 160.5 %reduce-scatter.2.cloned.1.call-start = ((), (), s32[]{:S(2)}) async-start(), calls=%async_computation.7 | async-start | bytes 9437184 | tf_op jit(solution)/shard_map/reduce_scatter | solution.py:111
  307.7 9.2 %copy-start.3 = (bf16[512,4096]{1,0:T(8,128)(2,1)S(1)}, bf16[512,4096]{1,0:T(8,128)(2,1)}, u32[]{:S(2)}) copy-start(bf16[512,4096]{1,0:T(8,128)(2,1)} %param.11) | copy-start | bytes 12582916
  311.3 5.6 %collective-permute-start.1 = (bf16[63,512]{1,0:T(8,128)(2,1)S(1)}, bf16[63,512]{1,0:T(8,128)(2,1)S(1)}, u32[]{:S(2)}, u32[]{:S(2)}) collective-permute-start(bf16[63,512]{1,0:T(8,128)(2,1)S(1)} %slice.30), channel_id=1, source_target_pairs={{0,8},{8,16},{16,24},{24,32},{32,40},{40,48},{48,56},{56,64},{64,7... | collective-permute-start | bytes 193544 | tf_op jit(solution)/shard_map/ppermute | solution.py:15
  315.6 98.4 %copy-start.4 = (bf16[512,512]{1,0:T(8,128)(2,1)S(1)}, bf16[512,512]{1,0:T(8,128)(2,1)}, u32[]{:S(2)}) copy-start(bf16[512,512]{1,0:T(8,128)(2,1)} %param.8) | copy-start | bytes 1572868
  316.9 99.5 %copy-start.1 = (bf16[8,128,512]{2,1,0:T(8,128)(2,1)S(1)}, bf16[8,128,512]{2,1,0:T(8,128)(2,1)}, u32[]{:S(2)}) copy-start(bf16[8,128,512]{2,1,0:T(8,128)(2,1)} %param.12) | copy-start | bytes 3145732
Sparse Core Ops, SparseCore 0:
  322.6 91.3 reduce-scatter.1
